TPU v7x, 32 devices: a whole 2x2x4 slice. The times are simulated.
32 devices in a mesh: replica: 8 (over z, core), shard: 4 (over y, x).
Axes of the slice: x: 2, y: 2, z: 4, core: 2. Of those that a mesh axis runs over, the one named last changes fastest.
Arguments:
- tokens: bfloat16 [32768, 2560], P(('replica', 'shard')), may hold values from -6 to 6
- w_in: bfloat16 [2560, 10496], P('shard'), may hold values from -0.125 to 0.125
- w_dt: bfloat16 [2560, 80], P('shard'), may hold values from -0.125 to 0.125
- w_out: bfloat16 [5120, 2560], P('shard'), may hold values from -0.078125 to 0.078125
- norm_gain: float32 [2560], replicated, may hold values from 0.5 to 1.5
- conv_weight: float32 [4, 5376], replicated, may hold values from -3 to 3
- conv_bias: float32 [5376], replicated, may hold values from -1.5 to 1.5
- dt_bias: float32 [80], replicated, may hold values from -5 to -1
- a_log: float32 [80], replicated, may hold values from -3 to 2.5
- d_skip: float32 [80], replicated, may hold values from 0.5 to 1.5
- gate_gain: float32 [5120], replicated, may hold values from 0.5 to 1.5
- cotangent: bfloat16 [32768, 2560], P(('replica', 'shard')), may hold values from -8 to 8
Outputs:
- result: bfloat16 [32768, 2560], P(('replica', 'shard'))
- token_grad: float32 [32768, 2560], P(('replica', 'shard'))
- grad_w_in: float32 [2560, 10496], P('shard')
- grad_w_dt: float32 [2560, 80], P('shard')
- grad_w_out: float32 [5120, 2560], P('shard')
- grad_norm_gain: float32 [2560], replicated
- grad_conv_weight: float32 [4, 5376], replicated
- grad_conv_bias: float32 [5376], replicated
- grad_dt_bias: float32 [80], replicated
- grad_a_log: float32 [80], replicated
- grad_d_skip: float32 [80], replicated
- grad_gate_gain: float32 [5120], replicated
All inputs are finite; a program needn't handle non-finite values.
Results may differ from a plain program's by a relative error of at most 0.017.
Values may be sent and summed in bfloat16 or wider, within the bound.
No kernel may reach another device: no remote copies, remote signals or barrier semaphores. Data moves between devices by JAX's collectives and lax.ppermute only.
A program may use at most 768 MiB of HBM per device.

v0:
```python
import jax
import jax.numpy as jnp
from jax import lax
from jax.sharding import PartitionSpec as P

H = 80
P_SIZE = 64
E = 5120
NST = 128
CONVK = 4
SPAN = 256
eps = 1e-05


def rms_norm(tokens_f, gain):
    return tokens_f * lax.rsqrt(jnp.mean(tokens_f * tokens_f, axis=-1, keepdims=True) + eps) * gain


def contract_rows(left, right):
    return lax.dot_general(
        left, right, (((0,), (0,)), ((), ())), preferred_element_type=jnp.float32
    )


def contract_cols(left, right):
    return lax.dot_general(
        left, right, (((1,), (1,)), ((), ())), preferred_element_type=jnp.float32
    )


def ssd_scan(values, step_size, log_decay, in_state, out_state):
    length = values.shape[0]
    blocks = length // SPAN
    highest = lax.Precision.HIGHEST
    values4 = values.reshape(blocks, SPAN, H, P_SIZE)
    decay_blk = log_decay.reshape(blocks, SPAN, H).transpose(0, 2, 1)
    step_blk = step_size.reshape(blocks, SPAN, H).transpose(0, 2, 1)
    in_blk = in_state.reshape(blocks, SPAN, NST)
    out_blk = out_state.reshape(blocks, SPAN, NST)
    running = jnp.cumsum(decay_blk, axis=2)
    gap = running[:, :, :, None] - running[:, :, None, :]
    lower = jnp.tril(jnp.ones((SPAN, SPAN), dtype=bool))
    weights = jnp.where(lower, jnp.exp(jnp.where(lower, gap, 0.0)), 0.0)
    intersection = jnp.einsum("bln,bsn->bls", out_blk, in_blk, precision=highest)
    scores = weights * intersection[:, None, :, :] * step_blk[:, :, None, :]
    inner = jnp.einsum("bhls,bshp->blhp", scores, values4, precision=highest)
    to_end = jnp.exp(running[:, :, -1:] - running) * step_blk
    local = jnp.einsum("bsn,bhs,bshp->bhpn", in_blk, to_end, values4, precision=highest)
    whole_decay = jnp.exp(running[:, :, -1])

    def carry_state(state, item):
        decay_now, add_now = item
        return (state * decay_now[:, None, None] + add_now, state)

    _, prior = lax.scan(carry_state, jnp.zeros_like(local[0]), (whole_decay, local))
    outer = jnp.einsum("bln,bhpn,bhl->blhp", out_blk, prior, jnp.exp(running), precision=highest)
    return (inner + outer).reshape(length, H, P_SIZE)


def mixer(project, dt_raw, conv_weight, conv_bias, dt_bias, a_log, d_skip, gate_gain):
    length = project.shape[0]
    gate_part = project[:, :E]
    conv_in = project[:, E:]
    padded = jnp.pad(conv_in, ((CONVK - 1, 0), (0, 0)))
    conv_out = conv_bias + padded[0:length] * conv_weight[0]
    for offset in range(1, CONVK):
        conv_out = conv_out + padded[offset : offset + length] * conv_weight[offset]
    activ = jax.nn.silu(conv_out)
    values = activ[:, :E].reshape(length, H, P_SIZE)
    in_state = activ[:, E : E + NST]
    out_state = activ[:, E + NST :]
    step_size = jax.nn.softplus(dt_raw + dt_bias)
    log_decay = -jnp.exp(a_log) * step_size
    mixed = ssd_scan(values, step_size, log_decay, in_state, out_state) + d_skip[:, None] * values
    gated = mixed.reshape(length, E) * jax.nn.silu(gate_part)
    return rms_norm(gated, gate_gain)


def body(
    tokens,
    w_in,
    w_dt,
    w_out,
    norm_gain,
    conv_weight,
    conv_bias,
    dt_bias,
    a_log,
    d_skip,
    gate_gain,
    cotangent,
):
    tokens_f = tokens.astype(jnp.float32)
    normed_f, norm_pull = jax.vjp(rms_norm, tokens_f, norm_gain)
    normed = normed_f.astype(jnp.bfloat16)
    pieces = (
        lax.all_gather(w_in, "shard", axis=0, tiled=True),
        lax.all_gather(w_dt, "shard", axis=0, tiled=True),
    )
    columns = normed
    project = jnp.dot(columns, pieces[0], preferred_element_type=jnp.float32)
    dt_raw = jnp.dot(columns, pieces[1], preferred_element_type=jnp.float32)
    gated_f, mixer_pull = jax.vjp(
        mixer, project, dt_raw, conv_weight, conv_bias, dt_bias, a_log, d_skip, gate_gain
    )
    gated = gated_f.astype(jnp.bfloat16)
    columns = gated
    mixed_out = jnp.dot(
        columns,
        lax.all_gather(w_out, "shard", axis=0, tiled=True),
        preferred_element_type=jnp.float32,
    )
    result = (tokens_f + mixed_out).astype(jnp.bfloat16)
    grad_out = lax.psum_scatter(
        contract_rows(gated, cotangent).astype(jnp.bfloat16),
        "shard",
        scatter_dimension=0,
        tiled=True,
    ).astype(jnp.float32)
    back_gated = contract_cols(cotangent, lax.all_gather(w_out, "shard", axis=0, tiled=True))
    pulled = mixer_pull(back_gated)
    back_proj = pulled[0].astype(jnp.bfloat16)
    back_dt = pulled[1].astype(jnp.bfloat16)
    grad_in, grad_dt = (
        lax.psum_scatter(
            contract_rows(normed, back_proj).astype(jnp.bfloat16),
            "shard",
            scatter_dimension=0,
            tiled=True,
        ).astype(jnp.float32),
        lax.psum_scatter(
            contract_rows(normed, back_dt).astype(jnp.bfloat16),
            "shard",
            scatter_dimension=0,
            tiled=True,
        ).astype(jnp.float32),
    )
    grad_in, grad_dt, grad_out = (
        lax.psum(grad_in.astype(jnp.bfloat16), "replica").astype(jnp.float32),
        lax.psum(grad_dt.astype(jnp.bfloat16), "replica").astype(jnp.float32),
        lax.psum(grad_out.astype(jnp.bfloat16), "replica").astype(jnp.float32),
    )
    pieces = (
        lax.all_gather(w_in, "shard", axis=0, tiled=True),
        lax.all_gather(w_dt, "shard", axis=0, tiled=True),
    )
    part_cols = contract_cols(back_proj, pieces[0]) + contract_cols(back_dt, pieces[1])
    back_tokens, grad_norm = norm_pull(part_cols)
    token_grad = cotangent.astype(jnp.float32) + back_tokens
    small_grads = lax.psum(
        (grad_norm, pulled[2], pulled[3], pulled[4], pulled[5], pulled[6], pulled[7]),
        ("replica", "shard"),
    )
    return (
        result,
        token_grad,
        grad_in,
        grad_dt,
        grad_out,
        small_grads[0],
        small_grads[1],
        small_grads[2],
        small_grads[3],
        small_grads[4],
        small_grads[5],
        small_grads[6],
    )


def solution(mesh):
    placed = (
        P(("replica", "shard"), None),
        P("shard", None),
        P("shard", None),
        P("shard", None),
        P(),
        P(),
        P(),
        P(),
        P(),
        P(),
        P(),
        P(("replica", "shard"), None),
    )
    return jax.shard_map(
        body,
        mesh=mesh,
        in_specs=placed,
        out_specs=(
            P(("replica", "shard"), None),
            P(("replica", "shard"), None),
            P("shard", None),
            P("shard", None),
            P("shard", None),
            P(),
            P(),
            P(),
            P(),
            P(),
            P(),
            P(),
        ),
        check_vma=False,
    )
```

profile of v0, /device:TPU:8, one launch (start us, length us, event | category | flops | bytes accessed | tf_op | source)
XLA Modules:
  0.0 2894.5 jit_solution(18246477915600876768)
XLA Ops:
  13.3 9.9 all_gather.13
  38.6 438.9 %all-gather.3.cloned.1.call-done = bf16[2560,10496]{1,0:T(8,128)(2,1)} async-done(((bf16[640,10496]{1,0:T(8,128)(2,1)}), bf16[2560,10496]{1,0:T(8,128)(2,1)}) %all-gather.3.cloned.1.call-update) | async-done | bytes 53739536 | tf_op jit(solution)/shard_map/all_gather | solution.py:97
  477.4 65.4 %fusion.87 = f32[1024,10496]{1,0:T(8,128)} fusion(bf16[2560,10496]{1,0:T(8,128)(2,1)} %all-gather.3.cloned.1.call-done, bf16[1024,2560]{1,0:T(8,128)(2,1)} %param.16, f32[2560]{0:T(1024)S(1)} %copy-done.54, f32[1024]{0:T(1024)S(1)} %fusion.78), kind=kOutput, calls=%fused_computation.169 | convolution fusion | flops 55039754240 | bytes 101988352 | tf_op jit(solution)/shard_map/dot_general | solution.py:101
  542.9 16.0 slice.71
  558.9 48.1 %fusion.26 = (f32[1024,5376]{1,0:T(8,128)}, f32[1024,5376]{1,0:T(8,128)}) fusion(f32[1024,5376]{1,0:T(8,128)} %slice.71, f32[5376]{0:T(1024)S(1)} %get-tuple-element.251, f32[5376]{0:T(1024)S(1)} %get-tuple-element.252, f32[5376]{0:T(1024)S(1)} %get-tuple-element.250, f32[5376]{0:T(1024)S(1)} %get-tuple-element.249, f32[5376]{0:T(1024)S(1)} %copy-done.62), kind=kLoop, calls=%fused_computation.51 | loop fusion | flops 66060288 | bytes 66167808 | tf_op jit(solution)/shard_map/jvp(jit(silu))/mul | solution.py:68
  607.0 16.4 slice.72
  623.4 21.5 copy.140
  644.9 25.4 reshape.217
  673.5 18.7 copy_multiply_fusion.1
  700.1 27.8 fusion.34
  727.9 17.7 while.34
  745.6 21.1 fusion.96
  773.9 103.0 %fusion.33 = f32[4,256,80,64]{1,3,2,0:T(8,128)} fusion(f32[4,80,64,256]{3,2,1,0:T(8,128)S(1)} %fusion.96, f32[4,256,80]{1,2,0:T(8,128)S(1)} %copy-done.12, f32[4,80,256]{2,1,0:T(8,128)S(1)} %bitcast.216, f32[4,256,256]{2,1,0:T(8,128)S(1)} %copy-done.23, f32[4,80,256]{2,1,0:T(8,128)S(1)} %copy-done.26, pred[256,256]{1,0:T(8,128)(4,1)S(1)} %copy-done.52, ...), kind=kOutput, calls=%fused_computation.61 | convolution fusion | flops 16221470720 | bytes 65011712 | tf_op jit(solution)/shard_map/jvp(bhls,bshp->blhp)/dot_general | solution.py:46
  876.8 34.0 %copy.189 = f32[4,256,80,64]{3,2,1,0:T(8,128)} copy(f32[4,256,80,64]{1,3,2,0:T(8,128)} %fusion.33) | data formatting | bytes 41943040 | tf_op jit(solution)/shard_map/jvp()/reshape | solution.py:57
  910.9 33.3 %reshape.248 = f32[1024,5120]{1,0:T(8,128)} reshape(f32[4,256,80,64]{3,2,1,0:T(8,128)} %copy.189) | data formatting | bytes 41943040 | tf_op jit(solution)/shard_map/jvp()/reshape | solution.py:57
  944.2 28.8 multiply_reduce_fusion.11
  973.0 37.9 %multiply_reduce_fusion.8 = (f32[5120]{0:T(1024)}, f32[1024]{0:T(1024)S(1)}, f32[1024,5120]{1,0:T(8,128)}) fusion(f32[1024,5120]{1,0:T(8,128)} %get-tuple-element.294, f32[1024]{0:T(1024)S(1)} %fusion.79, f32[5120]{0:T(1024)S(1)} %copy-done.63, bf16[1024,2560]{1,0:T(8,128)(2,1)} %param.27, bf16[5120,2560]{1,0:T(8,128)(2,1)} %all-gather.5.cloned.1.call-done), kind=kOutput, calls=%fused_computation.68 | convolution fusion | flops 26874998784 | bytes 73449472 | tf_op jit(solution)/shard_map/dot_general | solution.py:26
  1010.9 50.2 %multiply_reduce_fusion.9 = (f32[5120]{0:T(1024)}, f32[1024,5120]{1,0:T(8,128)}, f32[1024,5120]{1,0:T(8,128)}) fusion(f32[1024,5376]{1,0:T(8,128)} %get-tuple-element.295, f32[1024,10496]{1,0:T(8,128)} %fusion.87, f32[1024,5120]{1,0:T(8,128)} %get-tuple-element.294, f32[1024]{0:T(1024)S(1)} %multiply_multiply_fusion.2, f32[1024]{0:T(1024)S(1)} %fusion.79, ...), kind=kLoop, calls=%fused_computation.69 | loop fusion | flops 110095360 | bytes 146870272 | tf_op jit(solution)/shard_map/transpose(jvp())/reduce_sum | solution.py:74
  1061.1 21.3 copy.152
  1082.4 25.4 reshape.225
  1107.9 27.8 fusion.29
  1135.7 136.2 %fusion.11 = (f32[4,80,256]{2,1,0:T(8,128)}, f32[4,80,256]{2,1,0:T(8,128)}, f32[4,80,256]{2,1,0:T(8,128)}, f32[4,256,256]{2,1,0:T(8,128)}) fusion(f32[4,80,256]{2,1,0:T(8,128)S(1)} %bitcast.217, f32[4,256,256]{2,1,0:T(8,128)S(1)} %copy-done.24, f32[4,80,256]{2,1,0:T(8,128)S(1)} %copy-done.27, pred[256,256]{1,0:T(8,128)(4,1)S(1)} %copy-done.53, ...), kind=kOutput, calls=%fused_computation.23 | convolution fusion | flops 16420192256 | bytes 45744128 | tf_op jit(solution)/shard_map/transpose(jvp(bhls,bshp->blhp))/dot_general | solution.py:46
  1271.9 76.8 %fusion.6 = f32[4,80,64,256]{3,2,1,0:T(8,128)} fusion(f32[4,80,256]{2,1,0:T(8,128)S(1)} %bitcast.218, f32[4,256,256]{2,1,0:T(8,128)S(1)} %copy-done.24, f32[4,80,256]{2,1,0:T(8,128)S(1)} %copy-done.27, pred[256,256]{1,0:T(8,128)(4,1)S(1)} %copy-done.53, f32[4,80,64,256]{3,0,2,1:T(4,128)S(1)} %bitcast.191), kind=kOutput, calls=%fused_computation.19 | convolution fusion | flops 16210984960 | bytes 43712512 | tf_op jit(solution)/shard_map/transpose(jvp(bhls,bshp->blhp))/dot_general | solution.py:46
  1348.7 31.5 %multiply_reduce_fusion.6 = f32[4,80,256]{2,0,1:T(4,128)} fusion(f32[4,80,256,64]{2,3,1,0:T(8,128)} %bitcast.195, f32[4,256,80,64]{1,0,3,2:T(4,128)S(1)} %copy-done), kind=kLoop, calls=%fused_computation.62 | loop fusion | flops 10403840 | bytes 42270720
  1385.2 36.5 %while.35 = (s32[]{:T(128)}, f32[80,64,128]{2,1,0:T(8,128)}, f32[4,80]{1,0:T(4,128)S(1)}, f32[4,80,64,128]{3,1,2,0:T(8,128)}, f32[4,80,64,128]{3,2,1,0:T(8,128)}...) while((s32[]{:T(128)}, f32[80,64,128]{2,1,0:T(8,128)}, ...), condition=%wide.region_10.11_spmd.clone, body=%wide.region_8.10_spmd.clone.sunk | while | flops 3276724 | bytes 18352148 | solution.py:55
  1421.9 34.9 %bitcast_add_fusion.2 = (f32[4,256,80,64]{1,2,3,0:T(8,128)}, f32[4,256,80,64]{1,2,3,0:T(8,128)}) fusion(f32[4,80,64,256]{3,2,1,0:T(8,128)} %fusion.6, f32[4,256,80]{1,2,0:T(8,128)S(1)} %copy-done.19, f32[4,256,128,1]{2,1,3,0:T(8,128)S(1)} %bitcast.204, f32[4,80,64,128]{3,1,2,0:T(8,128)} %get-tuple-element.189), kind=kOutput, calls=%fused_computation.55 | convolution fusion | flops 8063549440 | bytes 74252288 | tf_op jit(solution)/shard_map/transpose(jvp(bsn,bhs,bshp->bhpn))/dot_general | solution.py:48
  1456.9 24.4 multiply_reduce_fusion.7
  1483.2 10.1 reduce-window.16
  1500.6 35.7 %convolution_convert_fusion.1 = bf16[5120,2560]{1,0:T(8,128)(2,1)} fusion(bf16[1024,2560]{1,0:T(8,128)(2,1)} %param.27, f32[1024,5120]{1,0:T(8,128)} %get-tuple-element.294, f32[5120]{0:T(1024)S(1)} %copy-done.64, f32[1024]{0:T(1024)S(1)} %copy-done.68), kind=kOutput, calls=%fused_computation.40 | convolution fusion | flops 26872381440 | bytes 52453376 | tf_op jit(solution)/shard_map/dot_general | solution.py:20
  1536.3 36.8 %copy.190 = f32[4,256,80,64]{3,2,1,0:T(8,128)} copy(f32[4,256,80,64]{1,2,3,0:T(8,128)} %get-tuple-element.316) | data formatting | bytes 41943040 | tf_op jit(solution)/shard_map/transpose(jvp())/reshape | solution.py:35
  1573.1 33.1 %reshape.249 = f32[1024,5120]{1,0:T(8,128)} reshape(f32[4,256,80,64]{3,2,1,0:T(8,128)} %copy.190) | data formatting | bytes 41943040 | tf_op jit(solution)/shard_map/transpose(jvp())/reshape | solution.py:35
  1606.3 40.5 %fusion.59 = f32[4,256,128]{2,1,0:T(8,128)S(1)} fusion(f32[4,80,64,128]{3,2,1,0:T(8,128)} %get-tuple-element.486, f32[4,256,80,64]{1,0,3,2:T(4,128)} %reshape.225, f32[4,256,80]{1,2,0:T(8,128)S(1)} %copy-done.14), kind=kOutput, calls=%fused_computation.111 | convolution fusion | flops 8058306560 | bytes 32309248 | tf_op jit(solution)/shard_map/transpose(jvp(bln,bhpn,bhl->blhp))/dot_general | solution.py:56
  1647.9 37.0 %convolution_bitcast_fusion = f32[4,256,128]{2,1,0:T(8,128)S(1)} fusion(f32[4,256,80,64]{1,2,3,0:T(8,128)} %copy-done.2, f32[4,80,64,128]{3,1,2,0:T(8,128)} %get-tuple-element.189), kind=kOutput, calls=%fused_computation.112 | convolution fusion | flops 8053063680 | bytes 31981568 | tf_op jit(solution)/shard_map/transpose(jvp(bsn,bhs,bshp->bhpn))/dot_general | solution.py:48
  1686.8 17.8 multiply_add_fusion.1
  1704.7 56.3 %multiply_reduce_fusion.4 = (f32[5376]{0:T(1024)S(1)}, f32[5376]{0:T(1024)S(1)}, f32[5376]{0:T(1024)S(1)}, f32[5376]{0:T(1024)}, f32[5376]{0:T(1024)S(1)}, /*index=5*/f32[1024,5376]{1,0:T(8,128)}) fusion(f32[1024,5376]{1,0:T(8,128)} %slice.71, f32[1024,10496]{1,0:T(8,128)} %fusion.87, f32[1024,5376]{1,0:T(8,128)} %get-tuple-element.296, ...), kind=kLoop, calls=%fused_computation.48 | loop fusion | flops 110073600 | bytes 110208000 | tf_op jit(solution)/shard_map/transpose(jvp())/reduce_sum | solution.py:67
  1760.9 34.7 %broadcast_multiply_fusion = (f32[1024,5376]{1,0:T(8,128)}, f32[1024,5376]{1,0:T(8,128)}, f32[1024,5376]{1,0:T(8,128)}, f32[1024,5376]{1,0:T(8,128)}) fusion(f32[1024,5376]{1,0:T(8,128)} %get-tuple-element.292, f32[5376]{0:T(1024)S(1)} %copy-done.41, f32[5376]{0:T(1024)S(1)} %copy-done.37, f32[5376]{0:T(1024)S(1)} %copy-done.39, f32[5376]{0:T(1024)S(1)} %copy-done.43), kind=kLoop, calls=%fused_computation.92 | loop fusion | flops 22020096 | bytes 110186496 | tf_op jit(solution)/shard_map/transpose(jvp())/mul | solution.py:67
  1795.6 36.1 %pad_add_fusion = f32[1024,5376]{1,0:T(8,128)} fusion(f32[1024,5376]{1,0:T(8,128)} %get-tuple-element.302, f32[1024,5376]{1,0:T(8,128)} %get-tuple-element.303, f32[1024,5376]{1,0:T(8,128)} %get-tuple-element.304, f32[1024,5376]{1,0:T(8,128)} %get-tuple-element.301), kind=kLoop, calls=%fused_computation.43 | loop fusion | flops 16515072 | bytes 110100480 | tf_op jit(solution)/shard_map/transpose(jvp())/add_any | solution.py:65
  1831.7 71.6 %convolution_convert_fusion = bf16[2560,10496]{1,0:T(8,128)(2,1)} fusion(f32[1024,5120]{1,0:T(8,128)} %get-tuple-element.300, f32[1024,5376]{1,0:T(8,128)} %pad_add_fusion, bf16[1024,2560]{1,0:T(8,128)(2,1)} %param.16, f32[2560]{0:T(1024)S(1)} %copy-done.56, f32[1024]{0:T(1024)S(1)} %copy-done.61), kind=kOutput, calls=%fused_computation.21 | convolution fusion | flops 55088119808 | bytes 101988352 | tf_op jit(solution)/shard_map/dot_general | solution.py:20
  1905.3 450.1 %reduce-scatter.6.cloned.1.call-done = bf16[640,10496]{1,0:T(8,128)(2,1)} async-done(((bf16[2560,10496]{1,0:T(8,128)(2,1)}), bf16[640,10496]{1,0:T(8,128)(2,1)}) %reduce-scatter.6.cloned.1.call-update) | async-done | bytes 13434896 | tf_op jit(solution)/shard_map/reduce_scatter | solution.py:125
  2355.5 72.5 %fusion.58 = f32[1024,2560]{1,0:T(8,128)} fusion(bf16[2560,10496]{1,0:T(8,128)(2,1)} %all-gather.3.cloned.1.call-done, f32[1024,5120]{1,0:T(8,128)} %get-tuple-element.300, f32[1024,5376]{1,0:T(8,128)} %pad_add_fusion), kind=kOutput, calls=%fused_computation.108 | convolution fusion | flops 55050764288 | bytes 107216896 | tf_op jit(solution)/shard_map/dot_general | solution.py:26
  2428.0 9.7 fusion.45
  2438.6 13.3 fusion.46
  2452.0 38.7 %fusion.48 = bf16[1024,2560]{1,0:T(8,128)(2,1)} fusion(bf16[1024,2560]{1,0:T(8,128)(2,1)S(1)} %bitcast.197, bf16[5120,2560]{1,0:T(8,128)(2,1)} %all-gather.5.cloned.1.call-done, f32[1024,5120]{1,0:T(8,128)} %get-tuple-element.294, f32[5120]{0:T(1024)S(1)} %copy-done.65, f32[1024]{0:T(1024)S(1)} %copy-done.69), kind=kOutput, calls=%fused_computation.100 | convolution fusion | flops 26867138560 | bytes 57696256 | tf_op jit(solution)/shard_map/dot_general | solution.py:108
  2491.0 42.3 %all-reduce.16 = (f32[2560]{0:T(1024)}, f32[5376]{0:T(1024)}, f32[80]{0:T(128)}, f32[80]{0:T(128)}, f32[80]{0:T(128)}, /*index=5*/f32[5120]{0:T(1024)}) all-reduce(f32[2560]{0:T(1024)S(1)} %get-tuple-element.247, f32[5376]{0:T(1024)S(1)} %copy-done.47, ...), channel_id=1, replica_groups=mesh['replica'=8,'shard'=4] {'replica','shard'}, use_global_device_ids=true, to_apply=%region_25.26 | all-reduce | flops 13296 | bytes 106368 | tf_op jit(solution)/shard_map/psum | solution.py:150
  2533.3 224.0 %all-reduce.23.cloned.1.call-done = (bf16[640,10496]{1,0:T(8,128)(2,1)}, bf16[640,80]{0,1:T(8,128)(2,1)}, bf16[1280,2560]{1,0:T(8,128)(2,1)}) async-done(((bf16[640,10496]{1,0:T(8,128)(2,1)}, bf16[640,80]{0,1:T(8,128)(2,1)}, bf16[1280,2560]{1,0:T(8,128)(2,1)}), (bf16[640,10496]{1,0:T(8,128)(2,1)}, bf16[640,80]{0,1:T(8,128)(2,1)}, bf16[1280,2560]{1,0:T(8,128)(2,1)})) %all-reduce.23.cloned.1.call-update) | async-done | bytes 20090896 | tf_op jit(solution)/shard_map/psum | solution.py:139
  2759.1 10.2 convert_element_type.59
  2769.3 9.3 convert_element_type.55
  2778.5 107.4 %all-reduce.21.cloned.1.call-done = f32[4,5376]{1,0:T(4,128)} async-done(((f32[4,5376]{1,0:T(4,128)}), f32[4,5376]{1,0:T(4,128)}) %all-reduce.21.cloned.1.call-update) | async-done | bytes 86032 | tf_op jit(solution)/shard_map/psum | solution.py:150
  (281 shorter events, 117.1 us)
Async XLA Ops:
  7.2 470.2 %all-gather.3.cloned.1.call-start = ((), (), s32[]{:S(2)}) async-start(), calls=%async_computation.3 | async-start | bytes 67174400 | tf_op jit(solution)/shard_map/all_gather | solution.py:97
  8.0 965.0 %all-gather.5.cloned.1.call-start = ((), (), s32[]{:S(2)}) async-start(), calls=%async_computation.4 | async-start | bytes 32768000 | tf_op jit(solution)/shard_map/all_gather | solution.py:110
  8.7 1894.8 %reduce-scatter.10.cloned.1.call-start = ((), (), s32[]{:S(2)}) async-start(), calls=%async_computation.8 | async-start | bytes 819200
  13.0 529.8 %copy-start.59 = (f32[1024]{0:T(1024)}, f32[1024]{0:T(1024)S(1)}, u32[]{:S(2)}) copy-start(f32[1024]{0:T(1024)S(1)} %fusion.78) | copy-start | bytes 12292
  13.3 545.6 %copy-start.36 = (f32[5376]{0:T(1024)}, f32[5376]{0:T(1024)S(1)}, u32[]{:S(2)}) copy-start(f32[5376]{0:T(1024)S(1)} %get-tuple-element.249) | copy-start | bytes 64516
  13.3 545.6 %copy-start.38 = (f32[5376]{0:T(1024)}, f32[5376]{0:T(1024)S(1)}, u32[]{:S(2)}) copy-start(f32[5376]{0:T(1024)S(1)} %get-tuple-element.250) | copy-start | bytes 64516
  13.3 545.6 %copy-start.40 = (f32[5376]{0:T(1024)}, f32[5376]{0:T(1024)S(1)}, u32[]{:S(2)}) copy-start(f32[5376]{0:T(1024)S(1)} %get-tuple-element.251) | copy-start | bytes 64516
  13.3 545.6 %copy-start.42 = (f32[5376]{0:T(1024)}, f32[5376]{0:T(1024)S(1)}, u32[]{:S(2)}) copy-start(f32[5376]{0:T(1024)S(1)} %get-tuple-element.252) | copy-start | bytes 64516
  30.6 512.3 %copy-start.15 = (f32[1024,80]{0,1:T(8,128)}, f32[1024,80]{0,1:T(8,128)S(1)}, u32[]{:S(2)}) copy-start(f32[1024,80]{0,1:T(8,128)S(1)} %get-tuple-element.312) | copy-start | bytes 983044
  33.3 509.6 %copy-start.10 = (f32[4,80,2,128]{3,1,2,0:T(8,128)}, f32[4,80,2,128]{3,1,2,0:T(8,128)S(1)}, u32[]{:S(2)}) copy-start(f32[4,80,2,128]{3,1,2,0:T(8,128)S(1)} %reduce-window.14) | copy-start | bytes 983044
  33.6 509.2 %copy-start.44 = (f32[4,80,2]{1,2,0:T(2,128)}, f32[4,80,2]{1,2,0:T(2,128)S(1)}, u32[]{:S(2)}) copy-start(f32[4,80,2]{1,2,0:T(2,128)S(1)} %copy.144) | copy-start | bytes 7684
  34.8 508.1 %copy-start.50 = (f32[4,80]{1,0:T(4,128)}, f32[4,80]{1,0:T(4,128)S(1)}, u32[]{:S(2)}) copy-start(f32[4,80]{1,0:T(4,128)S(1)} %slice_reduce_fusion) | copy-start | bytes 3844
  671.6 74.1 %copy-start.5 = (f32[1024,128]{1,0:T(8,128)}, f32[1024,128]{1,0:T(8,128)S(1)}, u32[]{:S(2)}) copy-start(f32[1024,128]{1,0:T(8,128)S(1)} %get-tuple-element.305) | copy-start | bytes 1572868
  973.0 37.9 %copy-start.67 = (f32[1024]{0:T(1024)}, f32[1024]{0:T(1024)S(1)}, u32[]{:S(2)}) copy-start(f32[1024]{0:T(1024)S(1)} %fusion.79) | copy-start | bytes 12292
  1385.2 36.5 %copy-start.51 = (f32[4,80]{1,0:T(4,128)S(1)}, f32[4,80]{1,0:T(4,128)}, u32[]{:S(2)}) copy-start(f32[4,80]{1,0:T(4,128)} %copy-done.50) | copy-start | bytes 3844
  1385.2 36.6 %copy-start.9 = (f32[1024,128]{1,0:T(8,128)S(1)}, f32[1024,128]{1,0:T(8,128)}, u32[]{:S(2)}) copy-start(f32[1024,128]{1,0:T(8,128)} %copy-done.8) | copy-start | bytes 1572868
  1385.2 36.6 %copy-start.19 = (f32[4,256,80]{1,2,0:T(8,128)S(1)}, f32[4,256,80]{1,2,0:T(8,128)}, u32[]{:S(2)}) copy-start(f32[4,256,80]{1,2,0:T(8,128)} %get-tuple-element.311) | copy-start | bytes 983044
  1456.8 36.9 %copy-start.32 = (f32[1024,80]{0,1:T(8,128)S(1)}, f32[1024,80]{0,1:T(8,128)}, u32[]{:S(2)}) copy-start(f32[1024,80]{0,1:T(8,128)} %get-tuple-element.314) | copy-start | bytes 983044
  1456.8 36.9 %copy-start.73 = (f32[80]{0:T(128)S(1)}, f32[80]{0:T(128)}, u32[]{:S(2)}) copy-start(f32[80]{0:T(128)} %copy-done.72) | copy-start | bytes 964
  1456.8 38.5 %copy-start.55 = (f32[2560]{0:T(1024)S(1)}, f32[2560]{0:T(1024)}, u32[]{:S(2)}) copy-start(f32[2560]{0:T(1024)} %param.20) | copy-start | bytes 30724
  1456.8 38.5 %copy-start.60 = (f32[1024]{0:T(1024)S(1)}, f32[1024]{0:T(1024)}, u32[]{:S(2)}) copy-start(f32[1024]{0:T(1024)} %copy-done.59) | copy-start | bytes 12292
  1456.8 43.8 %copy-start.64 = (f32[5120]{0:T(1024)S(1)}, f32[5120]{0:T(1024)}, u32[]{:S(2)}) copy-start(f32[5120]{0:T(1024)} %param.26) | copy-start | bytes 61444
  1456.8 43.8 %copy-start.68 = (f32[1024]{0:T(1024)S(1)}, f32[1024]{0:T(1024)}, u32[]{:S(2)}) copy-start(f32[1024]{0:T(1024)} %copy-done.67) | copy-start | bytes 12292
  1500.5 404.7 %reduce-scatter.8.cloned.1.call-start = ((), (), s32[]{:S(2)}) async-start(), calls=%async_computation.6 | async-start | bytes 32768000 | tf_op jit(solution)/shard_map/reduce_scatter | solution.py:114
  1536.3 819.1 %reduce-scatter.6.cloned.1.call-start = ((), (), s32[]{:S(2)}) async-start(), calls=%async_computation.5 | async-start | bytes 67174400 | tf_op jit(solution)/shard_map/reduce_scatter | solution.py:125
  1606.3 40.5 %copy-start.17 = (f32[4,256,256]{2,1,0:T(8,128)S(1)}, f32[4,256,256]{2,1,0:T(8,128)}, u32[]{:S(2)}) copy-start(f32[4,256,256]{2,1,0:T(8,128)} %get-tuple-element.239) | copy-start | bytes 3145732
  1606.3 80.5 %slice-start = ((s8[20971520]{0:T(1024)(128)(4,1)}), s8[4194304]{0:T(1024)(128)(4,1)S(1)}, s32[]{:S(2)}) async-start(s8[20971520]{0:T(1024)(128)(4,1)} %bitcast.192), calls=%async_computation.10 | async-start | bytes 8388608
  1606.3 80.5 %slice-start.1 = ((s8[20971520]{0:T(1024)(128)(4,1)}), s8[4194304]{0:T(1024)(128)(4,1)S(1)}, s32[]{:S(2)}) async-start(s8[20971520]{0:T(1024)(128)(4,1)} %bitcast.192), calls=%async_computation.11 | async-start | bytes 8388608
  1606.3 80.5 %slice-start.2 = ((s8[20971520]{0:T(1024)(128)(4,1)}), s8[4194304]{0:T(1024)(128)(4,1)S(1)}, s32[]{:S(2)}) async-start(s8[20971520]{0:T(1024)(128)(4,1)} %bitcast.192), calls=%async_computation.12 | async-start | bytes 8388608
  1606.3 80.5 %slice-start.3 = ((s8[20971520]{0:T(1024)(128)(4,1)}), s8[4194304]{0:T(1024)(128)(4,1)S(1)}, s32[]{:S(2)}) async-start(s8[20971520]{0:T(1024)(128)(4,1)} %bitcast.192), calls=%async_computation.13 | async-start | bytes 8388608
  1646.8 38.1 %copy-start.7 = (f32[1024,128]{1,0:T(8,128)S(1)}, f32[1024,128]{1,0:T(8,128)}, u32[]{:S(2)}) copy-start(f32[1024,128]{1,0:T(8,128)} %copy-done.5) | copy-start | bytes 1572868
  1646.8 40.0 %copy-start.31 = (f32[5120]{0:T(1024)S(1)}, f32[5120]{0:T(1024)}, u32[]{:S(2)}) copy-start(f32[5120]{0:T(1024)} %mul.410) | copy-start | bytes 61444
  1647.9 38.9 %slice-start.4 = ((s8[20971520]{0:T(1024)(128)(4,1)}), s8[4194304]{0:T(1024)(128)(4,1)S(1)}, s32[]{:S(2)}) async-start(s8[20971520]{0:T(1024)(128)(4,1)} %bitcast.192), calls=%async_computation.14 | async-start | bytes 8388608
  1704.6 56.3 %copy-start.37 = (f32[5376]{0:T(1024)S(1)}, f32[5376]{0:T(1024)}, u32[]{:S(2)}) copy-start(f32[5376]{0:T(1024)} %copy-done.36) | copy-start | bytes 64516
  1704.6 56.3 %copy-start.39 = (f32[5376]{0:T(1024)S(1)}, f32[5376]{0:T(1024)}, u32[]{:S(2)}) copy-start(f32[5376]{0:T(1024)} %copy-done.38) | copy-start | bytes 64516
  1704.6 56.3 %copy-start.41 = (f32[5376]{0:T(1024)S(1)}, f32[5376]{0:T(1024)}, u32[]{:S(2)}) copy-start(f32[5376]{0:T(1024)} %copy-done.40) | copy-start | bytes 64516
  1704.6 56.3 %copy-start.43 = (f32[5376]{0:T(1024)S(1)}, f32[5376]{0:T(1024)}, u32[]{:S(2)}) copy-start(f32[5376]{0:T(1024)} %copy-done.42) | copy-start | bytes 64516
  1795.6 36.1 %copy-start.61 = (f32[1024]{0:T(1024)S(1)}, f32[1024]{0:T(1024)}, u32[]{:S(2)}) copy-start(f32[1024]{0:T(1024)} %copy-done.59) | copy-start | bytes 12292
  1903.4 853.9 %all-reduce.23.cloned.1.call-start = ((), (), s32[]{:S(2)}) async-start(), calls=%async_computation.9 | async-start | bytes 40181760 | tf_op jit(solution)/shard_map/psum | solution.py:139
  2355.4 72.6 %copy-start.21 = (bf16[2560,80]{0,1:T(8,128)(2,1)S(1)}, bf16[2560,80]{0,1:T(8,128)(2,1)}, u32[]{:S(2)}) copy-start(bf16[2560,80]{0,1:T(8,128)(2,1)} %copy-done.20) | copy-start | bytes 1228804
  2355.4 72.6 %copy-start.29 = (bf16[1024,80]{0,1:T(8,128)(2,1)S(1)}, bf16[1024,80]{0,1:T(8,128)(2,1)}, u32[]{:S(2)}) copy-start(bf16[1024,80]{0,1:T(8,128)(2,1)} %copy-done.28) | copy-start | bytes 491524
  2355.4 530.4 %all-reduce.21.cloned.1.call-start = ((), (), s32[]{:S(2)}) async-start(), calls=%async_computation.7 | async-start | bytes 172032 | tf_op jit(solution)/shard_map/psum | solution.py:150
  2451.9 38.8 %copy-start.74 = (f32[80]{0:T(128)S(1)}, f32[80]{0:T(128)}, u32[]{:S(2)}) copy-start(f32[80]{0:T(128)} %get-tuple-element.309) | copy-start | bytes 964
  2451.9 38.8 %copy-start.77 = (f32[80]{0:T(128)S(1)}, f32[80]{0:T(128)}, u32[]{:S(2)}) copy-start(f32[80]{0:T(128)} %param.24) | copy-start | bytes 964
  2452.0 38.8 %copy-start.49 = (f32[5120]{0:T(1024)S(1)}, f32[5120]{0:T(1024)}, u32[]{:S(2)}) copy-start(f32[5120]{0:T(1024)} %get-tuple-element.288) | copy-start | bytes 61444
  2452.0 39.0 %copy-start.47 = (f32[5376]{0:T(1024)S(1)}, f32[5376]{0:T(1024)}, u32[]{:S(2)}) copy-start(f32[5376]{0:T(1024)} %get-tuple-element.245) | copy-start | bytes 64516
  2452.0 39.0 %copy-start.66 = (f32[5120]{0:T(1024)S(1)}, f32[5120]{0:T(1024)}, u32[]{:S(2)}) copy-start(f32[5120]{0:T(1024)} %get-tuple-element.243) | copy-start | bytes 61444
  2452.0 39.0 %copy-start.70 = (f32[80]{0:T(128)S(1)}, f32[80]{0:T(128)}, u32[]{:S(2)}) copy-start(f32[80]{0:T(128)} %get-tuple-element.290) | copy-start | bytes 964
  (44 other events, 934.8 us)
Sparse Core Ops, SparseCore 0:
  9.9 467.4 all-gather.2
  479.3 236.3 all-gather.4
  1500.7 25.7 reduce-scatter.9
  1536.4 230.6 reduce-scatter.7
  1903.5 451.8 reduce-scatter.5
  2358.9 398.3 all-reduce.22
  2763.5 122.3 all-reduce.20
where the time goes:
time: 2900 us; the launch traced here: 2890 us
  waiting for transfers between devices  1220 us (42%)
  matrix products  853 us (29%)
  other arithmetic  441 us (15%)
  local copies, waits for them, and re-layouts  311 us (11%)
  blocking collectives  52.3 us (2%)
    reduce_scatter x1, waiting for transfers between devices, body(): lax.psum_scatter(contract_rows(normed, back_proj).astype(jnp.bfloat16), '...  450 us
    all_gather x1, waiting for transfers between devices, body(): lax.all_gather(w_in, 'shard', axis=0, tiled=True)  439 us
    dot_general x3, matrix products, ssd_scan(): inner = jnp.einsum('bhls,bshp->blhp', scores, values4, precision=highest)  316 us
    psum x1, waiting for transfers between devices, body(): lax.psum(grad_in.astype(jnp.bfloat16), 'replica').astype(jnp.float32)  224 us
    dot_general x3, matrix products, contract_cols(): lax.dot_general(left, right, (((1,), (1,)), ((), ())), preferred_element_...  120 us
    dot_general x3, matrix products, contract_rows(): lax.dot_general(left, right, (((0,), (0,)), ((), ())), preferred_element_...  111 us
    psum x1, waiting for transfers between devices, body(): lax.psum((grad_norm, pulled[2], pulled[3], pulled[4], pulled[5], pulled[6...  107 us
    dot_general x3, matrix products, ssd_scan(): jnp.einsum('bsn,bhs,bshp->bhpn', in_blk, to_end, values4, precision=highest)  99.6 us
  transfers between devices with their start and end apart: 7, of which 4 were waited for; matrix products, arithmetic and copies ran while one was open for 37% of the time, Pallas kernels for 0%

commit v1 on v0

--- a/solution.py
+++ b/solution.py
@@ -10,6 +10,27 @@
 CONVK = 4
 SPAN = 256
 eps = 1e-05
+
+
+def collect(value, axis, dim):
+    size, index, rows = (lax.axis_size(axis), lax.axis_index(axis), value.shape[dim])
+    forward = [(i, (i + 1) % size) for i in range(size)]
+    behind = [(i, (i - 1) % size) for i in range(size)]
+    result = jnp.zeros((*value.shape[:dim], size * rows, *value.shape[dim + 1 :]), value.dtype)
+    result = lax.dynamic_update_slice_in_dim(result, value, index * rows, axis=dim)
+    from_left = from_right = value
+    halfway = size // 2
+    for step in range(1, halfway + 1):
+        from_left = lax.ppermute(from_left, axis, forward)
+        result = lax.dynamic_update_slice_in_dim(
+            result, from_left, (index - step) % size * rows, axis=dim
+        )
+        if step < size - halfway:
+            from_right = lax.ppermute(from_right, axis, behind)
+            result = lax.dynamic_update_slice_in_dim(
+                result, from_right, (index + step) % size * rows, axis=dim
+            )
+    return result
 
 
 def rms_norm(tokens_f, gain):
@@ -93,10 +114,7 @@
     tokens_f = tokens.astype(jnp.float32)
     normed_f, norm_pull = jax.vjp(rms_norm, tokens_f, norm_gain)
     normed = normed_f.astype(jnp.bfloat16)
-    pieces = (
-        lax.all_gather(w_in, "shard", axis=0, tiled=True),
-        lax.all_gather(w_dt, "shard", axis=0, tiled=True),
-    )
+    pieces = (collect(w_in, "shard", 0), lax.all_gather(w_dt, "shard", axis=0, tiled=True))
     columns = normed
     project = jnp.dot(columns, pieces[0], preferred_element_type=jnp.float32)
     dt_raw = jnp.dot(columns, pieces[1], preferred_element_type=jnp.float32)

time: 2900 us -> 4050 us (1.40)
  blocking collectives: 52.3 us -> 830 us
  waiting for transfers between devices: 1220 us -> 1540 us
  local copies, waits for them, and re-layouts: 311 us -> 376 us
    all_gather x1, blocking collectives: 9.92 us -> 789 us  [body(): lax.all_gather(w_dt, 'shard', axis=0, tiled=True)]
    ppermute x0 -> x3, waiting for transfers between devices: none -> 290 us  [the longest x2 290 us: collect(): from_left = lax.ppermute(from_left, axis, forward)]
    psum x1, waiting for transfers between devices: 224 us -> 273 us  [body(): lax.psum(grad_in.astype(jnp.bfloat16), 'replica').astype(jnp.float32)]
    dynamic_update_slice x0 -> x4, local copies, waits for them, and re-layouts: none -> 43.4 us  [the longest x2 24.6 us: collect(): lax.dynamic_update_slice_in_dim(result, from_left, (index - step) % size...]
  transfers between devices with their start and end apart: 7 -> 10, of which waited for: 4 -> 5; matrix products, arithmetic and copies ran while one was open for 37% -> 28% of each run, Pallas kernels for 0% -> 0%
where the time goes in v1:
time: 4050 us; the launch traced here: 4040 us
  waiting for transfers between devices  1540 us (38%)
  matrix products  849 us (21%)
  blocking collectives  830 us (20%)
  other arithmetic  423 us (10%)
  local copies, waits for them, and re-layouts  376 us (9%)
    all_gather x1, blocking collectives, body(): lax.all_gather(w_dt, 'shard', axis=0, tiled=True)  789 us
    reduce_scatter x1, waiting for transfers between devices, body(): lax.psum_scatter(contract_rows(normed, back_proj).astype(jnp.bfloat16), '...  450 us
    all_gather x1, waiting for transfers between devices, body(): lax.all_gather(w_in, 'shard', axis=0, tiled=True)  425 us
    dot_general x3, matrix products, ssd_scan(): inner = jnp.einsum('bhls,bshp->blhp', scores, values4, precision=highest)  316 us
    ppermute x2, waiting for transfers between devices, collect(): from_left = lax.ppermute(from_left, axis, forward)  290 us
    psum x1, waiting for transfers between devices, body(): lax.psum(grad_in.astype(jnp.bfloat16), 'replica').astype(jnp.float32)  273 us
    dot_general x3, matrix products, contract_cols(): lax.dot_general(left, right, (((1,), (1,)), ((), ())), preferred_element_...  118 us
    dot_general x3, matrix products, contract_rows(): lax.dot_general(left, right, (((0,), (0,)), ((), ())), preferred_element_...  112 us
  transfers between devices with their start and end apart: 10, of which 5 were waited for; matrix products, arithmetic and copies ran while one was open for 28% of the time, Pallas kernels for 0%

profile of v1, /device:TPU:8, one launch (start us, length us, event | category | flops | bytes accessed | tf_op | source)
XLA Modules:
  0.0 4041.1 jit_solution(13452432687074736653)
XLA Ops:
  10.2 289.8 %collective-permute-done = bf16[640,10496]{1,0:T(8,128)(2,1)} collective-permute-done((bf16[640,10496]{1,0:T(8,128)(2,1)}, bf16[640,10496]{1,0:T(8,128)(2,1)}, u32[]{:S(2)}, u32[]{:S(2)}) %collective-permute-start) | collective-permute-done | bytes 13434912 | tf_op jit(solution)/shard_map/ppermute | solution.py:24
  300.8 788.8 %all_gather.11 = bf16[2560,80]{0,1:T(8,128)(2,1)S(1)} all-gather(bf16[640,80]{0,1:T(8,128)(2,1)} %param.18), channel_id=1, replica_groups=mesh['replica'=8,'shard'=4] {'shard'}, dimensions={0}, use_global_device_ids=true | all-gather | bytes 512000 | tf_op jit(solution)/shard_map/all_gather | solution.py:117
  1107.9 20.0 broadcast_in_dim.85
  1146.1 12.9 constant_dynamic-update-slice_fusion.2
  1159.0 12.3 constant_dynamic-update-slice_fusion.1
  1171.4 63.9 %fusion.87 = f32[1024,10496]{1,0:T(8,128)} fusion(bf16[2560,10496]{1,0:T(8,128)(2,1)} %constant_dynamic-update-slice_fusion.1, bf16[1024,2560]{1,0:T(8,128)(2,1)S(1)} %bitcast.199, f32[2560]{0:T(1024)S(1)} %copy-done.58, f32[1024]{0:T(1024)S(1)} %fusion.78), kind=kOutput, calls=%fused_computation.173 | convolution fusion | flops 55039754240 | bytes 101988352 | tf_op jit(solution)/shard_map/dot_general | solution.py:119
  1235.3 16.0 slice.71
  1251.4 44.3 %fusion.26 = (f32[1024,5376]{1,0:T(8,128)}, f32[1024,5376]{1,0:T(8,128)}) fusion(f32[1024,5376]{1,0:T(8,128)} %slice.71, f32[5376]{0:T(1024)S(1)} %copy-done.44, f32[5376]{0:T(1024)S(1)} %copy-done.46, f32[5376]{0:T(1024)S(1)} %copy-done.42, f32[5376]{0:T(1024)S(1)} %copy-done.40, f32[5376]{0:T(1024)S(1)} %copy-done.68), kind=kLoop, calls=%fused_computation.51 | loop fusion | flops 66060288 | bytes 66167808 | tf_op jit(solution)/shard_map/jvp(jit(silu))/mul | solution.py:89
  1295.6 16.3 slice.72
  1311.9 21.4 copy.140
  1333.3 25.8 reshape.217
  1362.4 18.5 copy_multiply_fusion.1
  1388.8 27.8 fusion.34
  1416.5 17.7 while.34
  1434.3 20.9 fusion.96
  1462.2 103.0 %fusion.33 = f32[4,256,80,64]{1,3,2,0:T(8,128)} fusion(f32[4,80,64,256]{3,2,1,0:T(8,128)S(1)} %fusion.96, f32[4,256,80]{1,2,0:T(8,128)S(1)} %copy-done.14, f32[4,80,256]{2,1,0:T(8,128)S(1)} %bitcast.220, f32[4,256,256]{2,1,0:T(8,128)S(1)} %copy-done.25, f32[4,80,256]{2,1,0:T(8,128)S(1)} %copy-done.28, pred[256,256]{1,0:T(8,128)(4,1)S(1)} %copy-done.56, ...), kind=kOutput, calls=%fused_computation.61 | convolution fusion | flops 16221470720 | bytes 65011712 | tf_op jit(solution)/shard_map/jvp(bhls,bshp->blhp)/dot_general | solution.py:67
  1565.2 33.9 copy.189
  1599.1 33.6 reshape.248
  1632.7 28.8 multiply_reduce_fusion.11
  1661.6 37.8 multiply_reduce_fusion.8
  1699.5 50.3 %multiply_reduce_fusion.9 = (f32[5120]{0:T(1024)}, f32[1024,5120]{1,0:T(8,128)}, f32[1024,5120]{1,0:T(8,128)}) fusion(f32[1024,5376]{1,0:T(8,128)} %get-tuple-element.295, f32[1024,10496]{1,0:T(8,128)} %fusion.87, f32[1024,5120]{1,0:T(8,128)} %get-tuple-element.294, f32[1024]{0:T(1024)S(1)} %multiply_multiply_fusion.2, f32[1024]{0:T(1024)S(1)} %fusion.79, ...), kind=kLoop, calls=%fused_computation.69 | loop fusion | flops 110095360 | bytes 146870272 | tf_op jit(solution)/shard_map/transpose(jvp())/reduce_sum | solution.py:95
  1749.7 21.3 copy.152
  1771.1 25.4 reshape.225
  1796.5 27.4 fusion.29
  1823.8 136.4 %fusion.11 = (f32[4,80,256]{2,1,0:T(8,128)}, f32[4,80,256]{2,1,0:T(8,128)}, f32[4,80,256]{2,1,0:T(8,128)}, f32[4,256,256]{2,1,0:T(8,128)}) fusion(f32[4,80,256]{2,1,0:T(8,128)S(1)} %bitcast.221, f32[4,256,256]{2,1,0:T(8,128)S(1)} %copy-done.26, f32[4,80,256]{2,1,0:T(8,128)S(1)} %copy-done.29, pred[256,256]{1,0:T(8,128)(4,1)S(1)} %copy-done.57, ...), kind=kOutput, calls=%fused_computation.23 | convolution fusion | flops 16420192256 | bytes 45744128 | tf_op jit(solution)/shard_map/transpose(jvp(bhls,bshp->blhp))/dot_general | solution.py:67
  1960.2 76.8 %fusion.6 = f32[4,80,64,256]{3,2,1,0:T(8,128)} fusion(f32[4,80,256]{2,1,0:T(8,128)S(1)} %bitcast.222, f32[4,256,256]{2,1,0:T(8,128)S(1)} %copy-done.26, f32[4,80,256]{2,1,0:T(8,128)S(1)} %copy-done.29, pred[256,256]{1,0:T(8,128)(4,1)S(1)} %copy-done.57, f32[4,80,64,256]{3,0,2,1:T(4,128)S(1)} %bitcast.191), kind=kOutput, calls=%fused_computation.19 | convolution fusion | flops 16210984960 | bytes 43712512 | tf_op jit(solution)/shard_map/transpose(jvp(bhls,bshp->blhp))/dot_general | solution.py:67
  2042.1 28.6 while.35
  2070.7 34.9 bitcast_add_fusion.2
  2105.6 24.3 multiply_reduce_fusion.7
  2130.6 30.4 multiply_reduce_fusion.6
  2179.0 35.8 convolution_convert_fusion.1
  2214.9 36.6 copy.190
  2251.5 32.8 reshape.249
  2284.4 40.4 %fusion.59 = f32[4,256,128]{2,1,0:T(8,128)S(1)} fusion(f32[4,80,64,128]{3,2,1,0:T(8,128)} %get-tuple-element.486, f32[4,256,80,64]{1,0,3,2:T(4,128)} %reshape.225, f32[4,256,80]{1,2,0:T(8,128)S(1)} %copy-done.16), kind=kOutput, calls=%fused_computation.111 | convolution fusion | flops 8058306560 | bytes 32309248 | tf_op jit(solution)/shard_map/transpose(jvp(bln,bhpn,bhl->blhp))/dot_general | solution.py:77
  2325.9 37.2 convolution_bitcast_fusion
  2365.1 17.7 multiply_add_fusion.1
  2382.8 56.5 %multiply_reduce_fusion.4 = (f32[5376]{0:T(1024)S(1)}, f32[5376]{0:T(1024)S(1)}, f32[5376]{0:T(1024)S(1)}, f32[5376]{0:T(1024)}, f32[5376]{0:T(1024)S(1)}, /*index=5*/f32[1024,5376]{1,0:T(8,128)}) fusion(f32[1024,5376]{1,0:T(8,128)} %slice.71, f32[1024,10496]{1,0:T(8,128)} %fusion.87, f32[1024,5376]{1,0:T(8,128)} %get-tuple-element.296, ...), kind=kLoop, calls=%fused_computation.48 | loop fusion | flops 110073600 | bytes 110208000 | tf_op jit(solution)/shard_map/transpose(jvp())/reduce_sum | solution.py:88
  2439.3 34.6 broadcast_multiply_fusion
  2473.9 36.2 pad_add_fusion
  2510.1 71.6 %convolution_convert_fusion = bf16[2560,10496]{1,0:T(8,128)(2,1)} fusion(f32[1024,5120]{1,0:T(8,128)} %get-tuple-element.300, f32[1024,5376]{1,0:T(8,128)} %pad_add_fusion, bf16[1024,2560]{1,0:T(8,128)(2,1)} %param.16, f32[2560]{0:T(1024)S(1)} %copy-done.60, f32[1024]{0:T(1024)S(1)} %copy-done.66), kind=kOutput, calls=%fused_computation.21 | convolution fusion | flops 55088119808 | bytes 101988352 | tf_op jit(solution)/shard_map/dot_general | solution.py:41
  2584.1 449.7 %reduce-scatter.6.cloned.1.call-done = bf16[640,10496]{1,0:T(8,128)(2,1)} async-done(((bf16[2560,10496]{1,0:T(8,128)(2,1)}), bf16[640,10496]{1,0:T(8,128)(2,1)}) %reduce-scatter.6.cloned.1.call-update) | async-done | bytes 13434896 | tf_op jit(solution)/shard_map/reduce_scatter | solution.py:143
  3036.0 41.4 %fusion.48 = bf16[1024,2560]{1,0:T(8,128)(2,1)} fusion(bf16[1024,2560]{1,0:T(8,128)(2,1)} %param.16, bf16[5120,2560]{1,0:T(8,128)(2,1)} %all-gather.3.cloned.1.call-done, f32[1024,5120]{1,0:T(8,128)} %get-tuple-element.294, f32[5120]{0:T(1024)S(1)} %copy-done.71, f32[1024]{0:T(1024)S(1)} %copy-done.75), kind=kOutput, calls=%fused_computation.100 | convolution fusion | flops 26867138560 | bytes 57696256 | tf_op jit(solution)/shard_map/dot_general | solution.py:126
  3077.4 424.6 %all-gather.5.cloned.1.call-done = bf16[2560,10496]{1,0:T(8,128)(2,1)} async-done(((bf16[640,10496]{1,0:T(8,128)(2,1)}), bf16[2560,10496]{1,0:T(8,128)(2,1)}) %all-gather.5.cloned.1.call-update) | async-done | bytes 53739536 | tf_op jit(solution)/shard_map/all_gather | solution.py:162
  3502.0 72.3 %fusion.58 = f32[1024,2560]{1,0:T(8,128)} fusion(bf16[2560,10496]{1,0:T(8,128)(2,1)} %all-gather.5.cloned.1.call-done, f32[1024,5120]{1,0:T(8,128)} %get-tuple-element.300, f32[1024,5376]{1,0:T(8,128)} %pad_add_fusion), kind=kOutput, calls=%fused_computation.108 | convolution fusion | flops 55050764288 | bytes 107216896 | tf_op jit(solution)/shard_map/dot_general | solution.py:47
  3589.6 41.6 %all-reduce.16 = (f32[2560]{0:T(1024)}, f32[5376]{0:T(1024)}, f32[80]{0:T(128)}, f32[80]{0:T(128)}, f32[80]{0:T(128)}, /*index=5*/f32[5120]{0:T(1024)}) all-reduce(f32[2560]{0:T(1024)S(1)} %get-tuple-element.247, f32[5376]{0:T(1024)S(1)} %copy-done.51, ...), channel_id=1, replica_groups=mesh['replica'=8,'shard'=4] {'replica','shard'}, use_global_device_ids=true, to_apply=%region_25.26 | all-reduce | flops 13296 | bytes 106368 | tf_op jit(solution)/shard_map/psum | solution.py:168
  3631.1 272.8 %all-reduce.23.cloned.1.call-done = (bf16[640,10496]{1,0:T(8,128)(2,1)}, bf16[640,80]{0,1:T(8,128)(2,1)}, bf16[1280,2560]{1,0:T(8,128)(2,1)}) async-done(((bf16[640,10496]{1,0:T(8,128)(2,1)}, bf16[640,80]{0,1:T(8,128)(2,1)}, bf16[1280,2560]{1,0:T(8,128)(2,1)}), (bf16[640,10496]{1,0:T(8,128)(2,1)}, bf16[640,80]{0,1:T(8,128)(2,1)}, bf16[1280,2560]{1,0:T(8,128)(2,1)})) %all-reduce.23.cloned.1.call-update) | async-done | bytes 20090896 | tf_op jit(solution)/shard_map/psum | solution.py:157
  3903.9 16.1 convert_element_type.55
  3927.5 105.0 %all-reduce.21.cloned.1.call-done = f32[4,5376]{1,0:T(4,128)} async-done(((f32[4,5376]{1,0:T(4,128)}), f32[4,5376]{1,0:T(4,128)}) %all-reduce.21.cloned.1.call-update) | async-done | bytes 86032 | tf_op jit(solution)/shard_map/psum | solution.py:168
  (320 shorter events, 159.3 us)
Async XLA Ops:
  7.2 1097.4 %copy-start.83 = (f32[80]{0:T(128)S(1)}, f32[80]{0:T(128)}, u32[]{:S(2)}) copy-start(f32[80]{0:T(128)} %param.25) | copy-start | bytes 964
  7.2 1098.8 %copy-start.52 = (f32[4,5376]{1,0:T(4,128)S(1)}, f32[4,5376]{1,0:T(4,128)}, u32[]{:S(2)}) copy-start(f32[4,5376]{1,0:T(4,128)} %param.21) | copy-start | bytes 258052
  7.2 1654.4 %all-gather.3.cloned.1.call-start = ((), (), s32[]{:S(2)}) async-start(), calls=%async_computation.3 | async-start | bytes 32768000 | tf_op jit(solution)/shard_map/all_gather | solution.py:128
  7.2 292.7 %collective-permute-start = (bf16[640,10496]{1,0:T(8,128)(2,1)}, bf16[640,10496]{1,0:T(8,128)(2,1)}, u32[]{:S(2)}, u32[]{:S(2)}) collective-permute-start(bf16[640,10496]{1,0:T(8,128)(2,1)} %param.17), channel_id=1, source_target_pairs={{0,1},{1,2},{2,3},{3,0},{4,5},{5,6},{6,7},{7,4},{8,9},{9,10},{10,1... | collective-permute-start | bytes 40304648 | tf_op jit(solution)/shard_map/ppermute | solution.py:24
  8.8 1137.3 %collective-permute-start.1 = (bf16[640,10496]{1,0:T(8,128)(2,1)}, bf16[640,10496]{1,0:T(8,128)(2,1)}, u32[]{:S(2)}, u32[]{:S(2)}) collective-permute-start(bf16[640,10496]{1,0:T(8,128)(2,1)} %param.17), channel_id=1, source_target_pairs={{0,3},{1,0},{2,1},{3,2},{4,7},{5,4},{6,5},{7,6},{8,11},{9,8},{10,9... | collective-permute-start | bytes 40304648 | tf_op jit(solution)/shard_map/ppermute | solution.py:29
  300.0 859.0 %collective-permute-start.2 = (bf16[640,10496]{1,0:T(8,128)(2,1)}, bf16[640,10496]{1,0:T(8,128)(2,1)}, u32[]{:S(2)}, u32[]{:S(2)}) collective-permute-start(bf16[640,10496]{1,0:T(8,128)(2,1)} %collective-permute-done), channel_id=1, source_target_pairs={{0,1},{1,2},{2,3},{3,0},{4,5},{5,6},{6,7},{7,4},{8,9},{9,10},{10,1... | collective-permute-start | bytes 40304648 | tf_op jit(solution)/shard_map/ppermute | solution.py:24
  300.6 2281.8 %reduce-scatter.10.cloned.1.call-start = ((), (), s32[]{:S(2)}) async-start(), calls=%async_computation.8 | async-start | bytes 819200
  1093.9 77.5 %copy-start.64 = (f32[1024]{0:T(1024)}, f32[1024]{0:T(1024)S(1)}, u32[]{:S(2)}) copy-start(f32[1024]{0:T(1024)S(1)} %fusion.78) | copy-start | bytes 12292
  1360.4 73.9 %copy-start.6 = (f32[1024,128]{1,0:T(8,128)}, f32[1024,128]{1,0:T(8,128)S(1)}, u32[]{:S(2)}) copy-start(f32[1024,128]{1,0:T(8,128)S(1)} %get-tuple-element.305) | copy-start | bytes 1572868
  1380.9 35.7 copy-start.1
  1380.9 35.6 copy-start.78
  1661.6 37.9 copy-start.73
  1960.2 81.8 %copy-start.4 = (f32[80,64,128]{2,1,0:T(8,128)S(1)}, f32[80,64,128]{2,1,0:T(8,128)}, u32[]{:S(2)}) copy-start(f32[80,64,128]{2,1,0:T(8,128)} %custom-call.1) | copy-start | bytes 7864324
  2130.5 41.5 %copy-start.34 = (f32[1024,80]{0,1:T(8,128)S(1)}, f32[1024,80]{0,1:T(8,128)}, u32[]{:S(2)}) copy-start(f32[1024,80]{0,1:T(8,128)} %get-tuple-element.314) | copy-start | bytes 983044
  2130.5 41.5 %copy-start.80 = (f32[80]{0:T(128)S(1)}, f32[80]{0:T(128)}, u32[]{:S(2)}) copy-start(f32[80]{0:T(128)} %copy-done.79) | copy-start | bytes 964
  2130.6 43.1 %copy-start.59 = (f32[2560]{0:T(1024)S(1)}, f32[2560]{0:T(1024)}, u32[]{:S(2)}) copy-start(f32[2560]{0:T(1024)} %param.20) | copy-start | bytes 30724
  2130.6 43.1 %copy-start.65 = (f32[1024]{0:T(1024)S(1)}, f32[1024]{0:T(1024)}, u32[]{:S(2)}) copy-start(f32[1024]{0:T(1024)} %copy-done.64) | copy-start | bytes 12292
  2130.6 48.4 %copy-start.70 = (f32[5120]{0:T(1024)S(1)}, f32[5120]{0:T(1024)}, u32[]{:S(2)}) copy-start(f32[5120]{0:T(1024)} %param.26) | copy-start | bytes 61444
  2130.6 48.4 %copy-start.74 = (f32[1024]{0:T(1024)S(1)}, f32[1024]{0:T(1024)}, u32[]{:S(2)}) copy-start(f32[1024]{0:T(1024)} %copy-done.73) | copy-start | bytes 12292
  2178.9 405.2 %reduce-scatter.8.cloned.1.call-start = ((), (), s32[]{:S(2)}) async-start(), calls=%async_computation.6 | async-start | bytes 32768000 | tf_op jit(solution)/shard_map/reduce_scatter | solution.py:132
  2214.8 819.0 %reduce-scatter.6.cloned.1.call-start = ((), (), s32[]{:S(2)}) async-start(), calls=%async_computation.5 | async-start | bytes 67174400 | tf_op jit(solution)/shard_map/reduce_scatter | solution.py:143
  2284.3 40.5 %copy-start.11 = (f32[1024,128]{1,0:T(8,128)S(1)}, f32[1024,128]{1,0:T(8,128)}, u32[]{:S(2)}) copy-start(f32[1024,128]{1,0:T(8,128)} %copy-done.9) | copy-start | bytes 1572868
  2284.3 40.5 %copy-start.20 = (f32[4,256,256]{2,1,0:T(8,128)S(1)}, f32[4,256,256]{2,1,0:T(8,128)}, u32[]{:S(2)}) copy-start(f32[4,256,256]{2,1,0:T(8,128)} %get-tuple-element.239) | copy-start | bytes 3145732
  2284.3 80.7 %slice-start = ((s8[20971520]{0:T(1024)(128)(4,1)}), s8[4194304]{0:T(1024)(128)(4,1)S(1)}, s32[]{:S(2)}) async-start(s8[20971520]{0:T(1024)(128)(4,1)} %bitcast.192), calls=%async_computation.10 | async-start | bytes 8388608
  2284.4 80.7 %slice-start.1 = ((s8[20971520]{0:T(1024)(128)(4,1)}), s8[4194304]{0:T(1024)(128)(4,1)S(1)}, s32[]{:S(2)}) async-start(s8[20971520]{0:T(1024)(128)(4,1)} %bitcast.192), calls=%async_computation.11 | async-start | bytes 8388608
  2284.4 80.7 %slice-start.2 = ((s8[20971520]{0:T(1024)(128)(4,1)}), s8[4194304]{0:T(1024)(128)(4,1)S(1)}, s32[]{:S(2)}) async-start(s8[20971520]{0:T(1024)(128)(4,1)} %bitcast.192), calls=%async_computation.12 | async-start | bytes 8388608
  2284.4 80.7 %slice-start.3 = ((s8[20971520]{0:T(1024)(128)(4,1)}), s8[4194304]{0:T(1024)(128)(4,1)S(1)}, s32[]{:S(2)}) async-start(s8[20971520]{0:T(1024)(128)(4,1)} %bitcast.192), calls=%async_computation.13 | async-start | bytes 8388608
  2324.8 38.3 copy-start.8
  2324.8 40.2 copy-start.33
  2325.9 39.1 slice-start.4
  2382.8 56.5 %copy-start.41 = (f32[5376]{0:T(1024)S(1)}, f32[5376]{0:T(1024)}, u32[]{:S(2)}) copy-start(f32[5376]{0:T(1024)} %get-tuple-element.249) | copy-start | bytes 64516
  2382.8 56.5 %copy-start.43 = (f32[5376]{0:T(1024)S(1)}, f32[5376]{0:T(1024)}, u32[]{:S(2)}) copy-start(f32[5376]{0:T(1024)} %get-tuple-element.250) | copy-start | bytes 64516
  2382.8 56.5 %copy-start.45 = (f32[5376]{0:T(1024)S(1)}, f32[5376]{0:T(1024)}, u32[]{:S(2)}) copy-start(f32[5376]{0:T(1024)} %get-tuple-element.251) | copy-start | bytes 64516
  2382.8 56.5 %copy-start.47 = (f32[5376]{0:T(1024)S(1)}, f32[5376]{0:T(1024)}, u32[]{:S(2)}) copy-start(f32[5376]{0:T(1024)} %get-tuple-element.252) | copy-start | bytes 64516
  2473.9 36.2 copy-start.60
  2473.9 36.2 copy-start.66
  2581.7 452.3 %copy-start.53 = (f32[5120]{0:T(1024)S(1)}, f32[5120]{0:T(1024)}, u32[]{:S(2)}) copy-start(f32[5120]{0:T(1024)} %get-tuple-element.288) | copy-start | bytes 61444
  2581.7 453.0 %copy-start.81 = (f32[80]{0:T(128)S(1)}, f32[80]{0:T(128)}, u32[]{:S(2)}) copy-start(f32[80]{0:T(128)} %get-tuple-element.309) | copy-start | bytes 964
  2581.7 453.0 %copy-start.84 = (f32[80]{0:T(128)S(1)}, f32[80]{0:T(128)}, u32[]{:S(2)}) copy-start(f32[80]{0:T(128)} %param.24) | copy-start | bytes 964
  2581.7 454.2 %copy-start.71 = (f32[5120]{0:T(1024)S(1)}, f32[5120]{0:T(1024)}, u32[]{:S(2)}) copy-start(f32[5120]{0:T(1024)} %param.26) | copy-start | bytes 61444
  2581.7 454.2 %copy-start.75 = (f32[1024]{0:T(1024)S(1)}, f32[1024]{0:T(1024)}, u32[]{:S(2)}) copy-start(f32[1024]{0:T(1024)} %copy-done.73) | copy-start | bytes 12292
  2581.7 920.3 %all-gather.5.cloned.1.call-start = ((), (), s32[]{:S(2)}) async-start(), calls=%async_computation.4 | async-start | bytes 67174400 | tf_op jit(solution)/shard_map/all_gather | solution.py:162
  2582.3 1321.6 %all-reduce.23.cloned.1.call-start = ((), (), s32[]{:S(2)}) async-start(), calls=%async_computation.9 | async-start | bytes 40181760 | tf_op jit(solution)/shard_map/psum | solution.py:157
  3033.8 998.7 %all-reduce.21.cloned.1.call-start = ((), (), s32[]{:S(2)}) async-start(), calls=%async_computation.7 | async-start | bytes 172032 | tf_op jit(solution)/shard_map/psum | solution.py:168
  3077.4 496.9 %copy-start.24 = (bf16[2560,80]{0,1:T(8,128)(2,1)S(1)}, bf16[2560,80]{0,1:T(8,128)(2,1)}, u32[]{:S(2)}) copy-start(bf16[2560,80]{0,1:T(8,128)(2,1)} %copy-done.23) | copy-start | bytes 1228804
  3077.4 496.9 %copy-start.31 = (bf16[1024,80]{0,1:T(8,128)(2,1)S(1)}, bf16[1024,80]{0,1:T(8,128)(2,1)}, u32[]{:S(2)}) copy-start(bf16[1024,80]{0,1:T(8,128)(2,1)} %copy-done.30) | copy-start | bytes 491524
  3077.4 496.9 %copy-start.61 = (f32[2560]{0:T(1024)S(1)}, f32[2560]{0:T(1024)}, u32[]{:S(2)}) copy-start(f32[2560]{0:T(1024)} %param.20) | copy-start | bytes 30724
  3077.4 496.9 %copy-start.67 = (f32[1024]{0:T(1024)S(1)}, f32[1024]{0:T(1024)}, u32[]{:S(2)}) copy-start(f32[1024]{0:T(1024)} %copy-done.64) | copy-start | bytes 12292
  (60 other events, 1205.7 us)
Sparse Core Ops, SparseCore 0:
  300.7 647.5 all-gather.2
  2179.0 25.7 reduce-scatter.9
  2215.0 230.6 reduce-scatter.7
  2581.8 451.9 reduce-scatter.5
  3035.7 466.2 all-gather.4
  3505.5 398.3 all-reduce.22
  3910.1 122.3 all-reduce.20
